TPU v7x, 128 devices: a whole 4x4x4 slice. The times are simulated.
128 devices in a mesh: slab: 16 (over z, x), pencil: 8 (over y, core).
Axes of the slice: x: 4, y: 4, z: 4, core: 2. Of those that a mesh axis runs over, the one named last changes fastest.
Arguments:
- a_blocks: float32 [256, 64, 20480], P('slab', 'pencil'), may hold values from -1 to 8, as said below
- col_codes: int32 [256, 64, 5], P('slab', 'pencil'), may hold values from 0 to 8, as said below
- agg_of: int32 [256, 64], P('slab', 'pencil'), may hold values from 0 to 2047, as said below
- test_vectors: float32 [256, 64, 2048], P('slab', 'pencil'), may hold values from -36 to 36
Outputs:
- relaxed: float32 [256, 64, 2048], P('slab', 'pencil')
- tiles: float32 [256, 64, 512], P('slab', 'pencil')
- products: float32 [256, 64, 2560], P('slab', 'pencil')
Inputs may be any that keep to these rules, and one draw needn't show every extreme that they name: `col_codes`: slot 0 of every block row is code 4, the block row itself; slots 1 to 4 hold different codes among the other eight of the 3 x 3 neighbourhood. `agg_of`: aggregate g is owned by device g // 16, devices numbered slab-major. On each device the block rows, in row-major order, form 64 groups of 2 consecutive block rows; all block rows of a group belong to aggregates of one owner, and the groups of one device go to different owners. Some owners receive a group from every device. `a_blocks`: the diagonal entries of every slot-0 block lie in [1.99, 8].
All inputs are finite; a program needn't handle non-finite values.
Results may differ from a plain program's by a relative error of at most 0.0003.
Values sent between devices are 32-bit elements; how exact they have to be, the bound alone decides.
A program may use at most 320 MiB of HBM per device.

v0:
```python
import math
import jax
import jax.numpy as jnp
from jax import lax
from jax.sharding import PartitionSpec as P

BLK = 64
NV = 32
NC = 8
KS = 5
ITERS = 2
OMEGA = 2.0 / 3.0
FULL_PRECISION = lax.Precision.HIGHEST


def with_halo(cells, sides, width):
    for axis, dim in sides:
        count = lax.axis_size(axis)
        ends = count - 1
        head = lax.slice_in_dim(cells, 0, width, axis=dim)
        tail = lax.slice_in_dim(cells, cells.shape[dim] - width, cells.shape[dim], axis=dim)
        cells = jnp.concatenate(
            [
                lax.ppermute(tail, axis, [(i, (i + 1) % count) for i in range(ends)]),
                cells,
                lax.ppermute(head, axis, [((i + 1) % count, i) for i in range(ends)]),
            ],
            axis=dim,
        )
    return cells


def coarse_modes(cells, coarse):
    centre = jnp.arange(cells, dtype=jnp.float32) + 0.5
    order = jnp.arange(coarse, dtype=jnp.float32)
    return jnp.cos(math.pi * centre[:, None] * order[None, :] / cells)


def solve_maps(coarse):
    gram = jnp.einsum("gkv,glv->gkl", coarse, coarse, precision=FULL_PRECISION)
    trace_sum = jnp.trace(gram, axis1=1, axis2=2)
    ridge = 0.1 * trace_sum / NC + 1e-06
    gram = gram + ridge[:, None, None] * jnp.eye(NC, dtype=jnp.float32)[None]
    lower = jnp.linalg.cholesky(gram)
    half_solved = jax.scipy.linalg.solve_triangular(lower, coarse, lower=True)
    solved = jax.scipy.linalg.solve_triangular(lower, half_solved, lower=True, trans=1)
    return jnp.swapaxes(solved, 1, 2)


def slot_index(col_codes):
    height, across_devices = (col_codes.shape[0], col_codes.shape[1])
    row_pos = jnp.arange(height, dtype=jnp.int32)[:, None, None] + col_codes // 3
    col_pos = jnp.arange(across_devices, dtype=jnp.int32)[None, :, None] + col_codes % 3
    return (row_pos * (across_devices + 2) + col_pos).reshape(-1)


def pick_rows(padded, flat_index, height, across_devices):
    features = padded.shape[2]
    flat = padded.reshape(padded.shape[0] * padded.shape[1], features)
    picked = jnp.take(flat, flat_index, axis=0)
    return picked.reshape(height, across_devices, KS, features)


def fit_slots(slot_coefficient, slot_ids, per_owner):
    members = (slot_ids[None, :] == jnp.arange(per_owner, dtype=jnp.int32)[:, None]).astype(
        jnp.float32
    )
    counts = jnp.sum(members, axis=1)
    summed = jnp.dot(
        members,
        slot_coefficient.reshape(slot_coefficient.shape[0], NC * NV),
        precision=FULL_PRECISION,
    )
    coarse = summed.reshape(per_owner, NC, NV) / jnp.maximum(counts, 1.0)[:, None, None]
    maps = solve_maps(coarse)
    return jnp.dot(members.T, maps.reshape(per_owner, NV * NC), precision=FULL_PRECISION)


def pack_slots(chosen_f, payload, group_list, capacity):
    flat = payload.reshape(group_list, capacity * payload.shape[1])
    packed = jnp.dot(chosen_f, flat, precision=FULL_PRECISION)
    return packed.reshape(chosen_f.shape[0], capacity, payload.shape[1])


def unpack_slots(chosen_f, received, block_rows):
    flat = received.reshape(received.shape[0], received.shape[1] * received.shape[2])
    return jnp.dot(chosen_f.T, flat, precision=FULL_PRECISION).reshape(
        block_rows, received.shape[2]
    )


def send_owner(payload, slot_ids):
    arrived, arrived_ids = (
        lax.all_to_all(payload, ("slab", "pencil"), split_axis=0, concat_axis=0, tiled=True),
        lax.all_to_all(slot_ids, ("slab", "pencil"), split_axis=0, concat_axis=0, tiled=True),
    )
    return (arrived, arrived_ids)


def send_back(payload):
    returned = lax.all_to_all(payload, ("slab", "pencil"), split_axis=0, concat_axis=0, tiled=True)
    return returned


def shards(a_blocks, col_codes, agg_of, test_vectors):
    height, across_devices = (agg_of.shape[0], agg_of.shape[1])
    n_slab = lax.axis_size("slab")
    n_pencil = lax.axis_size("pencil")
    devices = n_slab * n_pencil
    blocks = a_blocks.reshape(height, across_devices, KS, BLK, BLK)
    diagonal = jnp.diagonal(blocks[:, :, 0], axis1=-2, axis2=-1)
    block_wide = jnp.transpose(blocks, (0, 1, 3, 2, 4)).reshape(
        height, across_devices, BLK, KS * BLK
    )
    flat_index = slot_index(col_codes)
    candidate_vectors = test_vectors.reshape(height, across_devices, BLK, NV)
    for sweep in range(ITERS):
        padded = with_halo(
            candidate_vectors.reshape(height, across_devices, BLK * NV),
            (("slab", 0), ("pencil", 1)),
            1,
        )
        picked = pick_rows(padded, flat_index, height, across_devices).reshape(
            height, across_devices, KS * BLK, NV
        )
        image = jnp.einsum("ijor,ijrw->ijow", block_wide, picked, precision=FULL_PRECISION)
        candidate_vectors = candidate_vectors - OMEGA * image / diagonal[:, :, :, None]
    squares = jnp.sum(candidate_vectors * candidate_vectors, axis=(0, 1, 2))
    totals = lax.psum(squares, ("slab", "pencil"))
    scale = jnp.sqrt(totals / (height * across_devices * BLK * devices) + 1e-06)
    relaxed = candidate_vectors / scale
    block_rows = height * across_devices
    capacity = 2 * block_rows // devices
    group_list = devices // 2
    per_owner = block_rows // 8
    near_null_modes = coarse_modes(BLK, NC)
    row_vectors = relaxed.reshape(block_rows, BLK, NV)
    group_agg = agg_of.reshape(group_list, capacity)
    group_owner = group_agg[:, 0] // per_owner
    chosen = group_owner[None, :] == jnp.arange(devices, dtype=jnp.int32)[:, None]
    chosen_f = chosen.astype(jnp.float32)
    slot_ids = (
        jnp.sum(jnp.where(chosen[:, :, None], group_agg[None] % per_owner + 1, 0), axis=1) - 1
    )
    slot_count = devices * capacity
    outgoing = pack_slots(chosen_f, row_vectors.reshape(block_rows, BLK * NV), group_list, capacity)
    arrived, arrived_ids = send_owner(outgoing, slot_ids)
    slot_vector_rows = arrived.reshape(slot_count, BLK, NV)
    slot_coefficient = jnp.einsum(
        "wd,xwf->xdf", near_null_modes, slot_vector_rows, precision=FULL_PRECISION
    )
    slot_maps = fit_slots(slot_coefficient, arrived_ids.reshape(slot_count), per_owner)
    slot_tiles = jnp.einsum(
        "scv,svk->sck",
        slot_vector_rows,
        slot_maps.reshape(slot_count, NV, NC),
        precision=FULL_PRECISION,
    )
    returned = send_back(slot_tiles.reshape(devices, capacity, BLK * NC))
    tile_rows = unpack_slots(chosen_f, returned, block_rows).reshape(block_rows, BLK, NC)
    tile_grid = tile_rows.reshape(height, across_devices, BLK * NC)
    padded_tiles = with_halo(tile_grid, (("slab", 0), ("pencil", 1)), 1)
    picked_tiles = pick_rows(padded_tiles, flat_index, height, across_devices).reshape(
        height, across_devices, KS, BLK, NC
    )
    products = jnp.einsum("ijkoc,ijkcw->ijkow", blocks, picked_tiles, precision=FULL_PRECISION)
    return (
        relaxed.reshape(height, across_devices, BLK * NV),
        tile_grid,
        products.reshape(height, across_devices, KS * BLK * NC),
    )


def solution(mesh):
    in_specs = (
        P("slab", "pencil", None),
        P("slab", "pencil", None),
        P("slab", "pencil"),
        P("slab", "pencil", None),
    )
    out_specs = (P("slab", "pencil", None), P("slab", "pencil", None), P("slab", "pencil", None))
    return jax.shard_map(shards, mesh=mesh, in_specs=in_specs, out_specs=out_specs, check_vma=False)
```

profile of v0, /device:TPU:7, one launch (start us, length us, event | category | flops | bytes accessed | tf_op | source)
XLA Modules:
  0.0 639.7 jit_solution(15918062208513373529)
XLA Ops:
  4.1 4.9 collective-permute-start
  11.9 38.9 %copy.177 = f32[16,8,20480]{0,1,2:T(8,128)} copy(f32[16,8,20480]{2,1,0:T(8,128)} %param.6) | data formatting | bytes 20971520 | tf_op args[0]
  50.9 11.6 %slice_bitcast_fusion = f32[16,8,64,64]{0,1,3,2:T(8,128)} fusion(f32[16,8,5,64,64]{0,1,4,3,2:T(8,128)} %bitcast), kind=kLoop, calls=%fused_computation.6 | loop fusion | bytes 4194304 | tf_op jit(solution)/shard_map/squeeze | solution.py:111
  76.0 6.4 %gather_fusion = f32[64,16,8]{1,2,0:T(8,128)S(1)} fusion(f32[16,8,64,64]{0,1,3,2:T(8,128)} %slice_bitcast_fusion, s32[64]{0:T(128)S(1)} %or_bitcast_fusion), kind=kCustom, calls=%fused_computation.2 | custom fusion | bytes 66048 | tf_op jit(solution)/shard_map/jit(diagonal)/gather | solution.py:111
  82.6 63.1 %copy.178 = f32[16,8,64,5,64]{2,4,3,1,0:T(8,128)} copy(f32[16,8,64,5,64]{0,1,4,2,3:T(8,128)} %bitcast.1) | data formatting | bytes 20971520 | tf_op jit(solution)/shard_map/transpose | solution.py:112
  150.0 4.6 gather_fusion.2
  154.6 5.2 broadcast_select_fusion.1
  159.8 13.7 %reshape_reshape.7 = f32[16,8,320,32]{3,2,1,0:T(8,128)} reshape(f32[640,2048]{1,0:T(8,128)} %broadcast_select_fusion.1) | data formatting | bytes 10485760 | tf_op jit(solution)/shard_map/reshape;reshape | solution.py:123
  173.5 37.9 %bitcast_subtract_fusion.1 = f32[16,8,64,32]{2,3,1,0:T(8,128)S(1)} fusion(f32[16,8,64,32]{2,3,1,0:T(8,128)} %copy.182, f32[16,8,320,32]{3,2,1,0:T(8,128)} %reshape_reshape.7, f32[16,8,64,320]{2,3,1,0:T(8,128)} %bitcast.82, f32[16,8,64]{2,1,0:T(8,128)S(1)} %copy.181), kind=kOutput, calls=%fused_computation.13 | convolution fusion | flops 1007419392 | bytes 17858560 | tf_op jit(solution)/shard_map/ijor,ijrw->ijow/dot_general | solution.py:126
  224.2 4.7 collective-permute-start.6
  231.6 10.5 %all-to-all-start.1 = ((s32[128,1,2]{2,1,0:T(1,128)}), s32[128,1,2]{2,1,0:T(1,128)S(1)}, u32[]{:S(2)}, u32[]{:S(2)}) async-start(s32[128,1,2]{2,1,0:T(1,128)} %copy.196), calls=%async_computation.1 | async-start | bytes 131072 | tf_op jit(solution)/shard_map/all_to_all | solution.py:95
  245.7 4.6 gather_fusion.3
  250.2 5.2 broadcast_select_fusion
  255.5 13.8 %reshape_reshape.8 = f32[16,8,320,32]{3,2,1,0:T(8,128)} reshape(f32[640,2048]{1,0:T(8,128)} %broadcast_select_fusion) | data formatting | bytes 10485760 | tf_op jit(solution)/shard_map/reshape;reshape | solution.py:123
  269.3 38.3 %multiply_reduce_fusion = (f32[32]{0:T(128)S(1)}, f32[16,8,64,32]{2,3,1,0:T(8,128)}) fusion(f32[16,8,64,32]{2,3,1,0:T(8,128)S(1)} %copy-done.1, f32[16,8,64]{2,1,0:T(8,128)S(1)} %copy.181, f32[16,8,320,32]{3,2,1,0:T(8,128)} %reshape_reshape.8, f32[16,8,64,320]{2,3,1,0:T(8,128)} %bitcast.83), kind=kOutput, calls=%fused_computation.14 | convolution fusion | flops 1007943680 | bytes 17858688 | tf_op jit(solution)/shard_map/ijor,ijrw->ijow/dot_general | solution.py:126
  307.6 65.2 %psum.7 = f32[32]{0:T(128)S(1)} all-reduce(f32[32]{0:T(128)S(1)} %get-tuple-element.33), channel_id=1, replica_groups=mesh['slab'=16,'pencil'=8] {'slab','pencil'}, use_global_device_ids=true, to_apply=%region_1.3 | all-reduce | flops 32 | bytes 256 | tf_op jit(solution)/shard_map/psum | solution.py:129
  385.2 7.3 %all-to-all-start = ((f32[128,2,2048]{2,1,0:T(2,128)}), f32[128,2,2048]{2,1,0:T(2,128)S(1)}, u32[]{:S(2)}, u32[]{:S(2)}) async-start(f32[128,2,2048]{2,1,0:T(2,128)} %copy.192), calls=%async_computation | async-start | bytes 4194304 | tf_op jit(solution)/shard_map/all_to_all | solution.py:94
  394.1 26.8 %all-to-all-done = f32[128,2,2048]{2,1,0:T(2,128)S(1)} async-done(((f32[128,2,2048]{2,1,0:T(2,128)}), f32[128,2,2048]{2,1,0:T(2,128)S(1)}, u32[]{:S(2)}, u32[]{:S(2)}) %all-to-all-start) | async-done | bytes 2097184 | tf_op jit(solution)/shard_map/all_to_all | solution.py:94
  421.0 5.3 reshape.246
  426.3 7.0 %copy.197 = f32[256,64,32]{0,1,2:T(8,128)S(1)} copy(f32[256,64,32]{2,1,0:T(8,128)} %reshape.246) | data formatting | bytes 4194304 | tf_op jit(solution)/shard_map/reshape | solution.py:148
  435.6 11.7 %custom-call.11 = f32[16,8,8]{2,1,0:T(8,128)S(1)} custom-call(f32[16,8,8]{2,1,0:T(8,128)S(1)} %fusion.18), custom_call_target="Cholesky" | custom-call | tf_op jit(solution)/shard_map/jit(cholesky)/cholesky | solution.py:44
  447.6 10.0 %custom-call.12 = f32[16,1,8,8]{2,3,1,0:T(8,128)S(1)} custom-call(f32[16,1,8,8]{3,2,1,0:T(8,128)S(1)} %select_bitcast_fusion), custom_call_target="InvertDiagBlocksLowerTriangular" | custom-call | tf_op jit(solution)/shard_map/jit(_solve_triangular)/vmap()/triangular_solve | solution.py:46
  459.0 11.2 %fusion.56 = f32[256,64,8]{2,1,0:T(8,128)} fusion(f32[256,64,32]{2,1,0:T(8,128)} %reshape.246, f32[256,32,8]{1,2,0:T(8,128)S(1)} %copy.209), kind=kOutput, calls=%fused_computation.114 | convolution fusion | flops 50331648 | bytes 2883584 | tf_op jit(solution)/shard_map/scv,svk->sck/dot_general | solution.py:153
  470.2 7.4 %reshape.249 = f32[128,2,512]{2,1,0:T(2,128)} reshape(f32[256,64,8]{2,1,0:T(8,128)} %fusion.56) | data formatting | bytes 1048576 | tf_op jit(solution)/shard_map/reshape | solution.py:159
  477.6 6.3 all-to-all-start.2
  484.1 11.8 %all-to-all-done.2 = f32[128,2,512]{2,1,0:T(2,128)S(1)} async-done(((f32[128,2,512]{2,1,0:T(2,128)}), f32[128,2,512]{2,1,0:T(2,128)S(1)}, u32[]{:S(2)}, u32[]{:S(2)}) %all-to-all-start.2) | async-done | bytes 524320 | tf_op jit(solution)/shard_map/all_to_all | solution.py:101
  502.2 4.6 collective-permute-done.9
  512.7 55.6 %copy.214 = f32[16,8,5,64,64]{4,3,2,1,0:T(8,128)} copy(f32[16,8,5,64,64]{0,1,4,3,2:T(8,128)} %bitcast) | data formatting | bytes 20971520 | tf_op jit(solution)/shard_map/reshape | solution.py:110
  575.2 13.6 %gather.15 = f32[16,8,5,64,8]{4,3,2,1,0:T(8,128)} reshape(f32[640,512]{1,0:T(8,128)S(1)} %gather_fusion.1) | data formatting | bytes 2621440 | tf_op jit(solution)/shard_map/jit(_take)/gather | solution.py:60
  588.8 37.9 %fusion.4 = f32[16,8,5,64,8]{3,4,2,1,0:T(8,128)S(1)} fusion(f32[16,8,5,64,64]{4,3,2,1,0:T(8,128)} %copy.214, f32[16,8,5,64,8]{4,3,2,1,0:T(8,128)} %gather.15, pred[16,8,5]{2,1,0:T(8,128)(4,1)S(1)} %copy.211), kind=kOutput, calls=%fused_computation.16 | convolution fusion | flops 251985920 | bytes 13107840 | tf_op jit(solution)/shard_map/ijkoc,ijkcw->ijkow/dot_general | solution.py:166
  626.7 6.0 copy.215
  632.7 6.8 %copy.216 = f32[16,8,2560]{2,1,0:T(8,128)} copy(f32[16,8,2560]{0,2,1:T(8,128)} %bitcast.84) | data formatting | bytes 2621440
  (128 shorter events, 80.2 us)
Async XLA Ops:
  1.6 61.6 %collective-permute-start.1 = (f32[1,8,2048]{2,0,1:T(1,128)S(1)}, f32[1,8,2048]{2,0,1:T(1,128)S(1)}, u32[]{:S(2)}, u32[]{:S(2)}) collective-permute-start(f32[1,8,2048]{2,0,1:T(1,128)S(1)} %copy.174), channel_id=1, source_target_pairs={{8,0},{16,8},{24,16},{32,24},{40,32},{48,40},{56,48},{64,56},{72,6... | collective-permute-start | bytes 196616 | tf_op jit(solution)/shard_map/ppermute | solution.py:26
  4.1 59.0 %collective-permute-start = (f32[1,8,2048]{2,0,1:T(1,128)S(1)}, f32[1,8,2048]{2,0,1:T(1,128)S(1)}, u32[]{:S(2)}, u32[]{:S(2)}) collective-permute-start(f32[1,8,2048]{2,0,1:T(1,128)S(1)} %copy.173), channel_id=1, source_target_pairs={{0,8},{8,16},{16,24},{24,32},{32,40},{40,48},{48,56},{56,64},{64,7... | collective-permute-start | bytes 196616 | tf_op jit(solution)/shard_map/ppermute | solution.py:24
  11.6 39.3 %copy-start.4 = (s32[16,8,5]{2,1,0:T(8,128)}, s32[16,8,5]{2,1,0:T(8,128)S(1)}, u32[]{:S(2)}) copy-start(s32[16,8,5]{2,1,0:T(8,128)S(1)} %copy.172) | copy-start | bytes 7684
  11.9 39.0 %copy-start.7 = (s32[64]{0:T(128)}, s32[64]{0:T(128)S(1)}, u32[]{:S(2)}) copy-start(s32[64]{0:T(128)S(1)} %and_select_fusion.1) | copy-start | bytes 772
  50.9 11.7 %copy-start.2 = (f32[16,8,2048]{2,1,0:T(8,128)S(1)}, f32[16,8,2048]{2,1,0:T(8,128)}, u32[]{:S(2)}) copy-start(f32[16,8,2048]{2,1,0:T(8,128)} %param.9) | copy-start | bytes 3145732
  63.2 82.5 %collective-permute-start.2 = (f32[18,1,2048]{2,0,1:T(8,128)S(1)}, f32[18,1,2048]{2,0,1:T(8,128)S(1)}, u32[]{:S(2)}, u32[]{:S(2)}) collective-permute-start(f32[18,1,2048]{2,0,1:T(8,128)S(1)} %get-tuple-element.25), channel_id=1, source_target_pairs={{0,1},{1,2},{2,3},{3,4},{4,5},{5,6},{6,7},{8,9},{9,10},{10,11},{11... | collective-permute-start | bytes 442376 | tf_op jit(solution)/shard_map/ppermute | solution.py:24
  67.6 78.2 %collective-permute-start.3 = (f32[18,1,2048]{2,0,1:T(8,128)S(1)}, f32[18,1,2048]{2,0,1:T(8,128)S(1)}, u32[]{:S(2)}, u32[]{:S(2)}) collective-permute-start(f32[18,1,2048]{2,0,1:T(8,128)S(1)} %get-tuple-element.26), channel_id=1, source_target_pairs={{1,0},{2,1},{3,2},{4,3},{5,4},{6,5},{7,6},{9,8},{10,9},{11,10},{12... | collective-permute-start | bytes 442376 | tf_op jit(solution)/shard_map/ppermute | solution.py:26
  211.4 5.2 copy-start
  211.7 12.2 %collective-permute-start.4 = (f32[1,8,2048]{2,1,0:T(8,128)S(1)}, f32[1,8,2048]{2,1,0:T(8,128)S(1)}, u32[]{:S(2)}, u32[]{:S(2)}) collective-permute-start(f32[1,8,2048]{2,1,0:T(8,128)S(1)} %slice.78), channel_id=1, source_target_pairs={{0,8},{8,16},{16,24},{24,32},{32,40},{40,48},{48,56},{56,64},{64,7... | collective-permute-start | bytes 196616 | tf_op jit(solution)/shard_map/ppermute | solution.py:24
  216.8 7.1 %collective-permute-start.5 = (f32[1,8,2048]{2,1,0:T(8,128)S(1)}, f32[1,8,2048]{2,1,0:T(8,128)S(1)}, u32[]{:S(2)}, u32[]{:S(2)}) collective-permute-start(f32[1,8,2048]{2,1,0:T(8,128)S(1)} %slice.80), channel_id=1, source_target_pairs={{8,0},{16,8},{24,16},{32,24},{40,32},{48,40},{56,48},{64,56},{72,6... | collective-permute-start | bytes 196616 | tf_op jit(solution)/shard_map/ppermute | solution.py:26
  224.2 18.0 %collective-permute-start.6 = (f32[18,1,2048]{2,1,0:T(1,128)S(1)}, f32[18,1,2048]{2,1,0:T(1,128)S(1)}, u32[]{:S(2)}, u32[]{:S(2)}) collective-permute-start(f32[18,1,2048]{2,1,0:T(1,128)S(1)} %get-tuple-element.23), channel_id=1, source_target_pairs={{0,1},{1,2},{2,3},{3,4},{4,5},{5,6},{6,7},{8,9},{9,10},{10,11},{11... | collective-permute-start | bytes 442376 | tf_op jit(solution)/shard_map/ppermute | solution.py:24
  228.9 13.2 %collective-permute-start.7 = (f32[18,1,2048]{2,1,0:T(1,128)S(1)}, f32[18,1,2048]{2,1,0:T(1,128)S(1)}, u32[]{:S(2)}, u32[]{:S(2)}) collective-permute-start(f32[18,1,2048]{2,1,0:T(1,128)S(1)} %get-tuple-element.24), channel_id=1, source_target_pairs={{1,0},{2,1},{3,2},{4,3},{5,4},{6,5},{7,6},{9,8},{10,9},{11,10},{12... | collective-permute-start | bytes 442376 | tf_op jit(solution)/shard_map/ppermute | solution.py:26
  231.6 153.6 %all-to-all-start.1 = ((s32[128,1,2]{2,1,0:T(1,128)}), s32[128,1,2]{2,1,0:T(1,128)S(1)}, u32[]{:S(2)}, u32[]{:S(2)}) async-start(s32[128,1,2]{2,1,0:T(1,128)} %copy.196), calls=%async_computation.1 | async-start | bytes 131072 | tf_op jit(solution)/shard_map/all_to_all | solution.py:95
  255.5 13.8 %copy-start.1 = (f32[16,8,64,32]{2,3,1,0:T(8,128)S(1)}, f32[16,8,64,32]{2,3,1,0:T(8,128)}, u32[]{:S(2)}) copy-start(f32[16,8,64,32]{2,3,1,0:T(8,128)} %copy-done) | copy-start | bytes 3145732
  377.6 3.5 copy-start.8
  385.2 35.8 %all-to-all-start = ((f32[128,2,2048]{2,1,0:T(2,128)}), f32[128,2,2048]{2,1,0:T(2,128)S(1)}, u32[]{:S(2)}, u32[]{:S(2)}) async-start(f32[128,2,2048]{2,1,0:T(2,128)} %copy.192), calls=%async_computation | async-start | bytes 4194304 | tf_op jit(solution)/shard_map/all_to_all | solution.py:94
  470.2 13.7 %copy-start.5 = (s32[16,8,5]{2,1,0:T(8,128)S(1)}, s32[16,8,5]{2,1,0:T(8,128)}, u32[]{:S(2)}) copy-start(s32[16,8,5]{2,1,0:T(8,128)} %copy-done.4) | copy-start | bytes 7684
  477.6 18.3 %all-to-all-start.2 = ((f32[128,2,512]{2,1,0:T(2,128)}), f32[128,2,512]{2,1,0:T(2,128)S(1)}, u32[]{:S(2)}, u32[]{:S(2)}) async-start(f32[128,2,512]{2,1,0:T(2,128)} %reshape.249), calls=%async_computation.2 | async-start | bytes 1048576 | tf_op jit(solution)/shard_map/all_to_all | solution.py:101
  496.3 5.8 collective-permute-start.8
  500.1 68.1 %copy-start.3 = (f32[16,8,512]{2,1,0:T(8,128)}, f32[16,8,512]{2,1,0:T(8,128)S(1)}, u32[]{:S(2)}) copy-start(f32[16,8,512]{2,1,0:T(8,128)S(1)} %reshape_reshape_reshape.7) | copy-start | bytes 786436
  500.2 6.6 %collective-permute-start.9 = (f32[1,8,512]{2,1,0:T(8,128)S(1)}, f32[1,8,512]{2,1,0:T(8,128)S(1)}, u32[]{:S(2)}, u32[]{:S(2)}) collective-permute-start(f32[1,8,512]{2,1,0:T(8,128)S(1)} %slice.87), channel_id=1, source_target_pairs={{8,0},{16,8},{24,16},{32,24},{40,32},{48,40},{56,48},{64,56},{72,6... | collective-permute-start | bytes 49160 | tf_op jit(solution)/shard_map/ppermute | solution.py:26
  506.8 66.1 %collective-permute-start.10 = (f32[18,1,512]{2,1,0:T(1,128)S(1)}, f32[18,1,512]{2,1,0:T(1,128)S(1)}, u32[]{:S(2)}, u32[]{:S(2)}) collective-permute-start(f32[18,1,512]{2,1,0:T(1,128)S(1)} %get-tuple-element.29), channel_id=1, source_target_pairs={{0,1},{1,2},{2,3},{3,4},{4,5},{5,6},{6,7},{8,9},{9,10},{10,11},{11... | collective-permute-start | bytes 110600 | tf_op jit(solution)/shard_map/ppermute | solution.py:24
  509.9 63.0 %collective-permute-start.11 = (f32[18,1,512]{2,1,0:T(1,128)S(1)}, f32[18,1,512]{2,1,0:T(1,128)S(1)}, u32[]{:S(2)}, u32[]{:S(2)}) collective-permute-start(f32[18,1,512]{2,1,0:T(1,128)S(1)} %get-tuple-element.30), channel_id=1, source_target_pairs={{1,0},{2,1},{3,2},{4,3},{5,4},{6,5},{7,6},{9,8},{10,9},{11,10},{12... | collective-permute-start | bytes 110600 | tf_op jit(solution)/shard_map/ppermute | solution.py:26
  512.7 55.6 %copy-start.6 = (pred[16,8,5]{0,1,2:T(8,128)(4,1)S(1)}, pred[16,8,5]{0,1,2:T(8,128)(4,1)}, u32[]{:S(2)}) copy-start(pred[16,8,5]{0,1,2:T(8,128)(4,1)} %get-tuple-element.19) | copy-start | bytes 1924
where the time goes:
time: 651 us; the launch traced here: 640 us
  local copies, waits for them, and re-layouts  300 us (46%)
  matrix products  130 us (20%)
  blocking collectives  65.2 us (10%)
  starting transfers between devices  61.2 us (9%)
  waiting for transfers between devices  43.2 us (7%)
  other arithmetic  39.2 us (6%)
    dot_general x2, matrix products, shards(): jnp.einsum('ijor,ijrw->ijow', block_wide, picked, precision=FULL_PRECISION)  76.2 us
    psum x1, blocking collectives, shards(): totals = lax.psum(squares, ('slab', 'pencil'))  65.2 us
    transpose x1, local copies, waits for them, and re-layouts, shards(): jnp.transpose(blocks, (0, 1, 3, 2, 4))  63.1 us
    reshape x1, local copies, waits for them, and re-layouts, shards(): blocks = a_blocks.reshape(height, across_devices, KS, BLK, BLK)  55.6 us
    unnamed x27, local copies, waits for them, and re-layouts  47.3 us
    dot_general x1, matrix products, shards(): jnp.einsum('ijkoc,ijkcw->ijkow', blocks, picked_tiles, precision=FULL_PRE...  37.9 us
    another operation x2, local copies, waits for them, and re-layouts, shards(): pick_rows(padded, flat_index, height, across_devices)  27.5 us
    all_to_all x1, waiting for transfers between devices, send_owner(): lax.all_to_all(payload, ('slab', 'pencil'), split_axis=0, concat_axis=0,...  26.8 us
  transfers between devices with their start and end apart: 15, of which 3 were waited for; matrix products, arithmetic and copies ran while one was open for 43% of the time, Pallas kernels for 0%

commit v1 on v0

--- a/solution.py
+++ b/solution.py
@@ -126,7 +126,7 @@
         image = jnp.einsum("ijor,ijrw->ijow", block_wide, picked, precision=FULL_PRECISION)
         candidate_vectors = candidate_vectors - OMEGA * image / diagonal[:, :, :, None]
     squares = jnp.sum(candidate_vectors * candidate_vectors, axis=(0, 1, 2))
-    totals = lax.psum(squares, ("slab", "pencil"))
+    totals = lax.psum(lax.psum(squares, "slab"), "pencil")
     scale = jnp.sqrt(totals / (height * across_devices * BLK * devices) + 1e-06)
     relaxed = candidate_vectors / scale
     block_rows = height * across_devices

time: 651 us -> 636 us (0.977)
  blocking collectives: 65.2 us -> 45.2 us
    psum x1 -> x2, blocking collectives: 65.2 us -> 45.2 us  [shards(): totals = lax.psum(lax.psum(squares, 'slab'), 'pencil')]
  transfers between devices with their start and end apart: 15 -> 15, of which waited for: 3 -> 3; matrix products, arithmetic and copies ran while one was open for 43% -> 44% of each run, Pallas kernels for 0% -> 0%
where the time goes in v1:
time: 636 us; the launch traced here: 625 us
  local copies, waits for them, and re-layouts  300 us (47%)
  matrix products  129 us (20%)
  starting transfers between devices  66.6 us (10%)
  blocking collectives  45.2 us (7%)
  waiting for transfers between devices  43.3 us (7%)
  other arithmetic  39.3 us (6%)
    dot_general x2, matrix products, shards(): jnp.einsum('ijor,ijrw->ijow', block_wide, picked, precision=FULL_PRECISION)  75.9 us
    transpose x1, local copies, waits for them, and re-layouts, shards(): jnp.transpose(blocks, (0, 1, 3, 2, 4))  63.1 us
    reshape x1, local copies, waits for them, and re-layouts, shards(): blocks = a_blocks.reshape(height, across_devices, KS, BLK, BLK)  55.7 us
    unnamed x27, local copies, waits for them, and re-layouts  47.3 us
    psum x2, blocking collectives, shards(): totals = lax.psum(lax.psum(squares, 'slab'), 'pencil')  45.2 us
    dot_general x1, matrix products, shards(): jnp.einsum('ijkoc,ijkcw->ijkow', blocks, picked_tiles, precision=FULL_PRE...  37.9 us
    another operation x2, local copies, waits for them, and re-layouts, shards(): pick_rows(padded, flat_index, height, across_devices)  27.5 us
    all_to_all x1, waiting for transfers between devices, send_owner(): lax.all_to_all(payload, ('slab', 'pencil'), split_axis=0, concat_axis=0,...  26.9 us
  transfers between devices with their start and end apart: 15, of which 3 were waited for; matrix products, arithmetic and copies ran while one was open for 44% of the time, Pallas kernels for 0%

profile of v1, /device:TPU:7, one launch (start us, length us, event | category | flops | bytes accessed | tf_op | source)
XLA Modules:
  0.0 625.1 jit_solution(5671844948510901150)
XLA Ops:
  4.1 4.9 collective-permute-start
  11.9 38.9 %copy.177 = f32[16,8,20480]{0,1,2:T(8,128)} copy(f32[16,8,20480]{2,1,0:T(8,128)} %param.6) | data formatting | bytes 20971520 | tf_op args[0]
  50.9 11.6 %slice_bitcast_fusion = f32[16,8,64,64]{0,1,3,2:T(8,128)} fusion(f32[16,8,5,64,64]{0,1,4,3,2:T(8,128)} %bitcast), kind=kLoop, calls=%fused_computation.6 | loop fusion | bytes 4194304 | tf_op jit(solution)/shard_map/squeeze | solution.py:111
  76.0 6.4 %gather_fusion = f32[64,16,8]{1,2,0:T(8,128)S(1)} fusion(f32[16,8,64,64]{0,1,3,2:T(8,128)} %slice_bitcast_fusion, s32[64]{0:T(128)S(1)} %or_bitcast_fusion), kind=kCustom, calls=%fused_computation.2 | custom fusion | bytes 66048 | tf_op jit(solution)/shard_map/jit(diagonal)/gather | solution.py:111
  82.6 63.1 %copy.178 = f32[16,8,64,5,64]{2,4,3,1,0:T(8,128)} copy(f32[16,8,64,5,64]{0,1,4,2,3:T(8,128)} %bitcast.1) | data formatting | bytes 20971520 | tf_op jit(solution)/shard_map/transpose | solution.py:112
  150.0 4.6 gather_fusion.2
  154.6 5.2 broadcast_select_fusion.1
  159.8 13.7 %reshape_reshape.7 = f32[16,8,320,32]{3,2,1,0:T(8,128)} reshape(f32[640,2048]{1,0:T(8,128)} %broadcast_select_fusion.1) | data formatting | bytes 10485760 | tf_op jit(solution)/shard_map/reshape;reshape | solution.py:123
  173.5 37.6 %bitcast_subtract_fusion.1 = f32[16,8,64,32]{2,3,1,0:T(8,128)S(1)} fusion(f32[16,8,64,32]{2,3,1,0:T(8,128)} %copy.182, f32[16,8,320,32]{3,2,1,0:T(8,128)} %reshape_reshape.7, f32[16,8,64,320]{2,3,1,0:T(8,128)} %bitcast.82, f32[16,8,64]{2,1,0:T(8,128)S(1)} %copy.181), kind=kOutput, calls=%fused_computation.13 | convolution fusion | flops 1007419392 | bytes 17858560 | tf_op jit(solution)/shard_map/ijor,ijrw->ijow/dot_general | solution.py:126
  223.9 4.7 collective-permute-start.6
  231.3 10.8 %all-to-all-start.1 = ((s32[128,1,2]{2,1,0:T(1,128)}), s32[128,1,2]{2,1,0:T(1,128)S(1)}, u32[]{:S(2)}, u32[]{:S(2)}) async-start(s32[128,1,2]{2,1,0:T(1,128)} %copy.196), calls=%async_computation.1 | async-start | bytes 131072 | tf_op jit(solution)/shard_map/all_to_all | solution.py:95
  250.2 5.2 broadcast_select_fusion
  255.4 13.8 %reshape_reshape.8 = f32[16,8,320,32]{3,2,1,0:T(8,128)} reshape(f32[640,2048]{1,0:T(8,128)} %broadcast_select_fusion) | data formatting | bytes 10485760 | tf_op jit(solution)/shard_map/reshape;reshape | solution.py:123
  269.2 38.3 %multiply_reduce_fusion = (f32[32]{0:T(128)S(1)}, f32[16,8,64,32]{2,3,1,0:T(8,128)}) fusion(f32[16,8,64,32]{2,3,1,0:T(8,128)S(1)} %copy-done.1, f32[16,8,64]{2,1,0:T(8,128)S(1)} %copy.181, f32[16,8,320,32]{3,2,1,0:T(8,128)} %reshape_reshape.8, f32[16,8,64,320]{2,3,1,0:T(8,128)} %bitcast.83), kind=kOutput, calls=%fused_computation.14 | convolution fusion | flops 1007943680 | bytes 17858688 | tf_op jit(solution)/shard_map/ijor,ijrw->ijow/dot_general | solution.py:126
  307.5 25.8 %psum.14 = f32[32]{0:T(128)S(1)} all-reduce(f32[32]{0:T(128)S(1)} %get-tuple-element.33), channel_id=1, replica_groups=mesh['slab'=16,'pencil'=8] {'slab'}, use_global_device_ids=true, to_apply=%region_1.3 | all-reduce | flops 32 | bytes 256 | tf_op jit(solution)/shard_map/psum | solution.py:129
  333.3 19.4 %psum.15 = f32[32]{0:T(128)S(1)} all-reduce(f32[32]{0:T(128)S(1)} %psum.14), channel_id=1, replica_groups=mesh['slab'=16,'pencil'=8] {'pencil'}, use_global_device_ids=true, to_apply=%region_2.4 | all-reduce | flops 32 | bytes 256 | tf_op jit(solution)/shard_map/psum | solution.py:129
  365.2 12.5 %all-to-all-start = ((f32[128,2,2048]{2,1,0:T(2,128)}), f32[128,2,2048]{2,1,0:T(2,128)S(1)}, u32[]{:S(2)}, u32[]{:S(2)}) async-start(f32[128,2,2048]{2,1,0:T(2,128)} %copy.192), calls=%async_computation | async-start | bytes 4194304 | tf_op jit(solution)/shard_map/all_to_all | solution.py:94
  379.3 26.9 %all-to-all-done = f32[128,2,2048]{2,1,0:T(2,128)S(1)} async-done(((f32[128,2,2048]{2,1,0:T(2,128)}), f32[128,2,2048]{2,1,0:T(2,128)S(1)}, u32[]{:S(2)}, u32[]{:S(2)}) %all-to-all-start) | async-done | bytes 2097184 | tf_op jit(solution)/shard_map/all_to_all | solution.py:94
  406.2 5.3 reshape.246
  411.6 7.0 %copy.197 = f32[256,64,32]{0,1,2:T(8,128)S(1)} copy(f32[256,64,32]{2,1,0:T(8,128)} %reshape.246) | data formatting | bytes 4194304 | tf_op jit(solution)/shard_map/reshape | solution.py:148
  420.8 11.7 %custom-call.11 = f32[16,8,8]{2,1,0:T(8,128)S(1)} custom-call(f32[16,8,8]{2,1,0:T(8,128)S(1)} %fusion.18), custom_call_target="Cholesky" | custom-call | tf_op jit(solution)/shard_map/jit(cholesky)/cholesky | solution.py:44
  432.8 10.0 %custom-call.12 = f32[16,1,8,8]{2,3,1,0:T(8,128)S(1)} custom-call(f32[16,1,8,8]{3,2,1,0:T(8,128)S(1)} %select_bitcast_fusion), custom_call_target="InvertDiagBlocksLowerTriangular" | custom-call | tf_op jit(solution)/shard_map/jit(_solve_triangular)/vmap()/triangular_solve | solution.py:46
  444.2 11.2 %fusion.56 = f32[256,64,8]{2,1,0:T(8,128)} fusion(f32[256,64,32]{2,1,0:T(8,128)} %reshape.246, f32[256,32,8]{1,2,0:T(8,128)S(1)} %copy.209), kind=kOutput, calls=%fused_computation.114 | convolution fusion | flops 50331648 | bytes 2883584 | tf_op jit(solution)/shard_map/scv,svk->sck/dot_general | solution.py:153
  455.4 7.4 %reshape.249 = f32[128,2,512]{2,1,0:T(2,128)} reshape(f32[256,64,8]{2,1,0:T(8,128)} %fusion.56) | data formatting | bytes 1048576 | tf_op jit(solution)/shard_map/reshape | solution.py:159
  462.8 6.3 %all-to-all-start.2 = ((f32[128,2,512]{2,1,0:T(2,128)}), f32[128,2,512]{2,1,0:T(2,128)S(1)}, u32[]{:S(2)}, u32[]{:S(2)}) async-start(f32[128,2,512]{2,1,0:T(2,128)} %reshape.249), calls=%async_computation.2 | async-start | bytes 1048576 | tf_op jit(solution)/shard_map/all_to_all | solution.py:101
  469.3 11.8 %all-to-all-done.2 = f32[128,2,512]{2,1,0:T(2,128)S(1)} async-done(((f32[128,2,512]{2,1,0:T(2,128)}), f32[128,2,512]{2,1,0:T(2,128)S(1)}, u32[]{:S(2)}, u32[]{:S(2)}) %all-to-all-start.2) | async-done | bytes 524320 | tf_op jit(solution)/shard_map/all_to_all | solution.py:101
  487.4 4.6 collective-permute-done.9
  497.9 55.7 %copy.214 = f32[16,8,5,64,64]{4,3,2,1,0:T(8,128)} copy(f32[16,8,5,64,64]{0,1,4,3,2:T(8,128)} %bitcast) | data formatting | bytes 20971520 | tf_op jit(solution)/shard_map/reshape | solution.py:110
  560.5 13.5 %gather.15 = f32[16,8,5,64,8]{4,3,2,1,0:T(8,128)} reshape(f32[640,512]{1,0:T(8,128)S(1)} %gather_fusion.1) | data formatting | bytes 2621440 | tf_op jit(solution)/shard_map/jit(_take)/gather | solution.py:60
  574.1 37.9 %fusion.4 = f32[16,8,5,64,8]{3,4,2,1,0:T(8,128)S(1)} fusion(f32[16,8,5,64,64]{4,3,2,1,0:T(8,128)} %copy.214, f32[16,8,5,64,8]{4,3,2,1,0:T(8,128)} %gather.15, pred[16,8,5]{2,1,0:T(8,128)(4,1)S(1)} %copy.211), kind=kOutput, calls=%fused_computation.16 | convolution fusion | flops 251985920 | bytes 13107840 | tf_op jit(solution)/shard_map/ijkoc,ijkcw->ijkow/dot_general | solution.py:166
  612.0 6.1 copy.215
  618.0 6.8 %copy.216 = f32[16,8,2560]{2,1,0:T(8,128)} copy(f32[16,8,2560]{0,2,1:T(8,128)} %bitcast.84) | data formatting | bytes 2621440
  (129 shorter events, 84.8 us)
Async XLA Ops:
  1.6 61.6 %collective-permute-start.1 = (f32[1,8,2048]{2,0,1:T(1,128)S(1)}, f32[1,8,2048]{2,0,1:T(1,128)S(1)}, u32[]{:S(2)}, u32[]{:S(2)}) collective-permute-start(f32[1,8,2048]{2,0,1:T(1,128)S(1)} %copy.174), channel_id=1, source_target_pairs={{8,0},{16,8},{24,16},{32,24},{40,32},{48,40},{56,48},{64,56},{72,6... | collective-permute-start | bytes 196616 | tf_op jit(solution)/shard_map/ppermute | solution.py:26
  4.1 59.0 %collective-permute-start = (f32[1,8,2048]{2,0,1:T(1,128)S(1)}, f32[1,8,2048]{2,0,1:T(1,128)S(1)}, u32[]{:S(2)}, u32[]{:S(2)}) collective-permute-start(f32[1,8,2048]{2,0,1:T(1,128)S(1)} %copy.173), channel_id=1, source_target_pairs={{0,8},{8,16},{16,24},{24,32},{32,40},{40,48},{48,56},{56,64},{64,7... | collective-permute-start | bytes 196616 | tf_op jit(solution)/shard_map/ppermute | solution.py:24
  11.6 39.3 %copy-start.4 = (s32[16,8,5]{2,1,0:T(8,128)}, s32[16,8,5]{2,1,0:T(8,128)S(1)}, u32[]{:S(2)}) copy-start(s32[16,8,5]{2,1,0:T(8,128)S(1)} %copy.172) | copy-start | bytes 7684
  11.9 39.0 %copy-start.7 = (s32[64]{0:T(128)}, s32[64]{0:T(128)S(1)}, u32[]{:S(2)}) copy-start(s32[64]{0:T(128)S(1)} %and_select_fusion.1) | copy-start | bytes 772
  50.9 11.7 %copy-start.2 = (f32[16,8,2048]{2,1,0:T(8,128)S(1)}, f32[16,8,2048]{2,1,0:T(8,128)}, u32[]{:S(2)}) copy-start(f32[16,8,2048]{2,1,0:T(8,128)} %param.9) | copy-start | bytes 3145732
  63.2 82.5 %collective-permute-start.2 = (f32[18,1,2048]{2,0,1:T(8,128)S(1)}, f32[18,1,2048]{2,0,1:T(8,128)S(1)}, u32[]{:S(2)}, u32[]{:S(2)}) collective-permute-start(f32[18,1,2048]{2,0,1:T(8,128)S(1)} %get-tuple-element.25), channel_id=1, source_target_pairs={{0,1},{1,2},{2,3},{3,4},{4,5},{5,6},{6,7},{8,9},{9,10},{10,11},{11... | collective-permute-start | bytes 442376 | tf_op jit(solution)/shard_map/ppermute | solution.py:24
  67.6 78.2 %collective-permute-start.3 = (f32[18,1,2048]{2,0,1:T(8,128)S(1)}, f32[18,1,2048]{2,0,1:T(8,128)S(1)}, u32[]{:S(2)}, u32[]{:S(2)}) collective-permute-start(f32[18,1,2048]{2,0,1:T(8,128)S(1)} %get-tuple-element.26), channel_id=1, source_target_pairs={{1,0},{2,1},{3,2},{4,3},{5,4},{6,5},{7,6},{9,8},{10,9},{11,10},{12... | collective-permute-start | bytes 442376 | tf_op jit(solution)/shard_map/ppermute | solution.py:26
  211.1 5.2 copy-start
  211.4 12.2 %collective-permute-start.4 = (f32[1,8,2048]{2,1,0:T(8,128)S(1)}, f32[1,8,2048]{2,1,0:T(8,128)S(1)}, u32[]{:S(2)}, u32[]{:S(2)}) collective-permute-start(f32[1,8,2048]{2,1,0:T(8,128)S(1)} %slice.78), channel_id=1, source_target_pairs={{0,8},{8,16},{16,24},{24,32},{32,40},{40,48},{48,56},{56,64},{64,7... | collective-permute-start | bytes 196616 | tf_op jit(solution)/shard_map/ppermute | solution.py:24
  216.5 7.1 %collective-permute-start.5 = (f32[1,8,2048]{2,1,0:T(8,128)S(1)}, f32[1,8,2048]{2,1,0:T(8,128)S(1)}, u32[]{:S(2)}, u32[]{:S(2)}) collective-permute-start(f32[1,8,2048]{2,1,0:T(8,128)S(1)} %slice.80), channel_id=1, source_target_pairs={{8,0},{16,8},{24,16},{32,24},{40,32},{48,40},{56,48},{64,56},{72,6... | collective-permute-start | bytes 196616 | tf_op jit(solution)/shard_map/ppermute | solution.py:26
  223.9 18.2 %collective-permute-start.6 = (f32[18,1,2048]{2,1,0:T(1,128)S(1)}, f32[18,1,2048]{2,1,0:T(1,128)S(1)}, u32[]{:S(2)}, u32[]{:S(2)}) collective-permute-start(f32[18,1,2048]{2,1,0:T(1,128)S(1)} %get-tuple-element.23), channel_id=1, source_target_pairs={{0,1},{1,2},{2,3},{3,4},{4,5},{5,6},{6,7},{8,9},{9,10},{10,11},{11... | collective-permute-start | bytes 442376 | tf_op jit(solution)/shard_map/ppermute | solution.py:24
  228.6 13.5 %collective-permute-start.7 = (f32[18,1,2048]{2,1,0:T(1,128)S(1)}, f32[18,1,2048]{2,1,0:T(1,128)S(1)}, u32[]{:S(2)}, u32[]{:S(2)}) collective-permute-start(f32[18,1,2048]{2,1,0:T(1,128)S(1)} %get-tuple-element.24), channel_id=1, source_target_pairs={{1,0},{2,1},{3,2},{4,3},{5,4},{6,5},{7,6},{9,8},{10,9},{11,10},{12... | collective-permute-start | bytes 442376 | tf_op jit(solution)/shard_map/ppermute | solution.py:26
  231.3 133.9 %all-to-all-start.1 = ((s32[128,1,2]{2,1,0:T(1,128)}), s32[128,1,2]{2,1,0:T(1,128)S(1)}, u32[]{:S(2)}, u32[]{:S(2)}) async-start(s32[128,1,2]{2,1,0:T(1,128)} %copy.196), calls=%async_computation.1 | async-start | bytes 131072 | tf_op jit(solution)/shard_map/all_to_all | solution.py:95
  255.4 13.8 %copy-start.1 = (f32[16,8,64,32]{2,3,1,0:T(8,128)S(1)}, f32[16,8,64,32]{2,3,1,0:T(8,128)}, u32[]{:S(2)}) copy-start(f32[16,8,64,32]{2,3,1,0:T(8,128)} %copy-done) | copy-start | bytes 3145732
  357.6 3.5 copy-start.8
  365.2 41.0 %all-to-all-start = ((f32[128,2,2048]{2,1,0:T(2,128)}), f32[128,2,2048]{2,1,0:T(2,128)S(1)}, u32[]{:S(2)}, u32[]{:S(2)}) async-start(f32[128,2,2048]{2,1,0:T(2,128)} %copy.192), calls=%async_computation | async-start | bytes 4194304 | tf_op jit(solution)/shard_map/all_to_all | solution.py:94
  455.4 13.7 %copy-start.5 = (s32[16,8,5]{2,1,0:T(8,128)S(1)}, s32[16,8,5]{2,1,0:T(8,128)}, u32[]{:S(2)}) copy-start(s32[16,8,5]{2,1,0:T(8,128)} %copy-done.4) | copy-start | bytes 7684
  462.8 18.3 %all-to-all-start.2 = ((f32[128,2,512]{2,1,0:T(2,128)}), f32[128,2,512]{2,1,0:T(2,128)S(1)}, u32[]{:S(2)}, u32[]{:S(2)}) async-start(f32[128,2,512]{2,1,0:T(2,128)} %reshape.249), calls=%async_computation.2 | async-start | bytes 1048576 | tf_op jit(solution)/shard_map/all_to_all | solution.py:101
  481.5 5.8 collective-permute-start.8
  485.4 68.2 %copy-start.3 = (f32[16,8,512]{2,1,0:T(8,128)}, f32[16,8,512]{2,1,0:T(8,128)S(1)}, u32[]{:S(2)}) copy-start(f32[16,8,512]{2,1,0:T(8,128)S(1)} %reshape_reshape_reshape.7) | copy-start | bytes 786436
  485.4 6.6 %collective-permute-start.9 = (f32[1,8,512]{2,1,0:T(8,128)S(1)}, f32[1,8,512]{2,1,0:T(8,128)S(1)}, u32[]{:S(2)}, u32[]{:S(2)}) collective-permute-start(f32[1,8,512]{2,1,0:T(8,128)S(1)} %slice.87), channel_id=1, source_target_pairs={{8,0},{16,8},{24,16},{32,24},{40,32},{48,40},{56,48},{64,56},{72,6... | collective-permute-start | bytes 49160 | tf_op jit(solution)/shard_map/ppermute | solution.py:26
  492.1 66.1 %collective-permute-start.10 = (f32[18,1,512]{2,1,0:T(1,128)S(1)}, f32[18,1,512]{2,1,0:T(1,128)S(1)}, u32[]{:S(2)}, u32[]{:S(2)}) collective-permute-start(f32[18,1,512]{2,1,0:T(1,128)S(1)} %get-tuple-element.29), channel_id=1, source_target_pairs={{0,1},{1,2},{2,3},{3,4},{4,5},{5,6},{6,7},{8,9},{9,10},{10,11},{11... | collective-permute-start | bytes 110600 | tf_op jit(solution)/shard_map/ppermute | solution.py:24
  495.1 63.0 %collective-permute-start.11 = (f32[18,1,512]{2,1,0:T(1,128)S(1)}, f32[18,1,512]{2,1,0:T(1,128)S(1)}, u32[]{:S(2)}, u32[]{:S(2)}) collective-permute-start(f32[18,1,512]{2,1,0:T(1,128)S(1)} %get-tuple-element.30), channel_id=1, source_target_pairs={{1,0},{2,1},{3,2},{4,3},{5,4},{6,5},{7,6},{9,8},{10,9},{11,10},{12... | collective-permute-start | bytes 110600 | tf_op jit(solution)/shard_map/ppermute | solution.py:26
  497.9 55.7 %copy-start.6 = (pred[16,8,5]{0,1,2:T(8,128)(4,1)S(1)}, pred[16,8,5]{0,1,2:T(8,128)(4,1)}, u32[]{:S(2)}) copy-start(pred[16,8,5]{0,1,2:T(8,128)(4,1)} %get-tuple-element.19) | copy-start | bytes 1924
